TPU v7x, 32 devices: a whole 2x2x4 slice. The times are simulated.
32 devices in a mesh: grp: 4 (over y, x), blk: 8 (over z, core).
Axes of the slice: x: 2, y: 2, z: 4, core: 2. Of those that a mesh axis runs over, the one named last changes fastest.
Arguments:
- queries: bfloat16 [4096, 1024], P(('grp', 'blk')), may hold values from -8 to 8
- key_rows: bfloat16 [4096, 128], P(('grp', 'blk')), may hold values from -8 to 8
- values: bfloat16 [4096, 128], P(('grp', 'blk')), may hold values from -6 to 6
- out_grad: bfloat16 [4096, 1024], P(('grp', 'blk')), may hold values from -6 to 6
- span_order: int32 [8], replicated, may hold values from 0 to 7, each once
Outputs:
- attended: bfloat16 [4096, 1024], P(('grp', 'blk'))
- grad_queries: bfloat16 [4096, 1024], P(('grp', 'blk'))
- grad_keys: bfloat16 [4096, 128], P(('grp', 'blk'))
- grad_values: bfloat16 [4096, 128], P(('grp', 'blk'))
Inputs may be any that keep to these rules, and one draw needn't show every extreme that they name: `span_order`: a permutation of 0 to 7.
All inputs are finite; a program needn't handle non-finite values.
Results may differ from a plain program's by a relative error of at most 0.015.
Values may be sent and summed in bfloat16 or wider, within the bound.
No kernel may reach another device: no remote copies, remote signals or barrier semaphores. Data moves between devices by JAX's collectives and lax.ppermute only.
A program may use at most 64 MiB of HBM per device.

v0:
```python
import math

import jax
import jax.numpy as jnp
from jax import lax
from jax.sharding import PartitionSpec as P

HEAD = 128


NEG_FILL = -1e30


def from_behind(block, axis, distance):
    devices = range(lax.axis_size(axis))
    route = [((i - distance) % len(devices), i) for i in devices]
    return lax.ppermute(block, axis, route)


def positions(span_order, grp_ids, blk_id, row_count, grp_count, blk_count):
    halfway = grp_count // 2
    columns = jnp.arange(blk_count, dtype=jnp.int32)
    lead_part = jnp.sum(jnp.where(columns == blk_id, span_order, 0))
    section = jnp.where(grp_ids < halfway, lead_part, 2 * blk_count - 1 - lead_part)
    inside = jnp.arange(row_count, dtype=jnp.int32)
    places = (
        section[:, None] * (halfway * row_count)
        + (grp_ids % halfway)[:, None] * row_count
        + inside[None, :]
    )
    return places.reshape(-1)


def masked_scores(query_head, key_head, query_pos, key_pos, factor):
    raw_scores = (
        jnp.einsum("qd,kd->qk", query_head, key_head, preferred_element_type=jnp.float32) * factor
    )
    visible = key_pos[None, :] <= query_pos[:, None]
    return (jnp.where(visible, raw_scores, NEG_FILL), visible)


def attend(query_rows, grad_rows, query_pos, kv_sets, key_pos_sets, sum_hook):
    head_dim = HEAD
    head_count = query_rows.shape[1] // head_dim
    query_count = query_rows.shape[0]
    factor = 1.0 / math.sqrt(head_dim)
    set_count = len(kv_sets)
    key_list = [member[:, :head_dim] for member in kv_sets]
    value_list = [member[:, head_dim:] for member in kv_sets]

    def column_of(matrix, head_idx):
        return lax.dynamic_slice_in_dim(matrix, head_idx * head_dim, head_dim, 1)

    maxima = jnp.zeros((query_count, head_count), jnp.float32)

    def forward_step(head_idx, running):
        blended, totals, found = running
        query_head = column_of(query_rows, head_idx)
        score_sets = [
            masked_scores(query_head, key_list[member], query_pos, key_pos_sets[member], factor)
            for member in range(set_count)
        ]
        row_top = jnp.full((query_count, 1), NEG_FILL, jnp.float32)
        for scores, visible in score_sets:
            row_top = jnp.maximum(row_top, jnp.max(scores, axis=1, keepdims=True))
        found = lax.dynamic_update_slice_in_dim(found, row_top, head_idx, 1)
        summed = jnp.zeros((query_count, head_dim), jnp.float32)
        row_total = jnp.zeros((query_count, 1), jnp.float32)
        for member in range(set_count):
            scores, visible = score_sets[member]
            weights = jnp.where(visible, jnp.exp(scores - row_top), 0.0)
            row_total = row_total + jnp.sum(weights, axis=1, keepdims=True)
            summed = summed + jnp.dot(
                weights.astype(jnp.bfloat16), value_list[member], preferred_element_type=jnp.float32
            )
        blended = lax.dynamic_update_slice_in_dim(blended, summed, head_idx * head_dim, 1)
        totals = lax.dynamic_update_slice_in_dim(totals, row_total, head_idx, 1)
        return (blended, totals, found)

    start_state = (
        jnp.zeros((query_count, head_count * head_dim), jnp.float32),
        jnp.zeros((query_count, head_count), jnp.float32),
        maxima,
    )
    blended, totals, maxima = lax.fori_loop(0, head_count, forward_step, start_state)
    blended, totals = sum_hook(blended, totals)
    out_heads = lax.optimization_barrier(
        (blended.reshape(query_count, head_count, head_dim) / totals[:, :, None]).astype(
            jnp.bfloat16
        )
    )
    grad_heads = grad_rows.reshape(query_count, head_count, head_dim)
    deltas = jnp.sum(grad_heads.astype(jnp.float32) * out_heads.astype(jnp.float32), axis=2)
    out_rows = out_heads.reshape(query_count, head_count * head_dim)

    def backward_step(head_idx, running):
        query_grad = running[0]
        query_head = column_of(query_rows, head_idx)
        grad_head = column_of(grad_rows, head_idx)
        row_top = lax.dynamic_slice_in_dim(maxima, head_idx, 1, 1)
        row_total = lax.dynamic_slice_in_dim(totals, head_idx, 1, 1)
        row_delta = lax.dynamic_slice_in_dim(deltas, head_idx, 1, 1)
        head_grad = jnp.zeros((query_count, head_dim), jnp.float32)
        updated = []
        for member in range(set_count):
            scores, visible = masked_scores(
                query_head, key_list[member], query_pos, key_pos_sets[member], factor
            )
            normed = jnp.where(visible, jnp.exp(scores - row_top), 0.0) / row_total
            value_grad = jnp.einsum(
                "qk,qd->kd",
                normed.astype(jnp.bfloat16),
                grad_head,
                preferred_element_type=jnp.float32,
            )
            prob_grad = jnp.einsum(
                "qd,kd->qk", grad_head, value_list[member], preferred_element_type=jnp.float32
            )
            score_grad = (normed * (prob_grad - row_delta)).astype(jnp.bfloat16)
            head_grad = head_grad + jnp.dot(
                score_grad, key_list[member], preferred_element_type=jnp.float32
            )
            key_grad = jnp.einsum(
                "qk,qd->kd", score_grad, query_head, preferred_element_type=jnp.float32
            )
            updated.append(running[1 + member] + jnp.concatenate([key_grad, value_grad], axis=1))
        query_grad = lax.dynamic_update_slice_in_dim(query_grad, head_grad, head_idx * head_dim, 1)
        return (query_grad,) + tuple(updated)

    start_grads = (jnp.zeros((query_count, head_count * head_dim), jnp.float32),) + tuple(
        (jnp.zeros((member.shape[0], 2 * head_dim), jnp.float32) for member in kv_sets)
    )
    finished = lax.fori_loop(0, head_count, backward_step, start_grads)
    query_grad = finished[0] * factor
    kv_grads = tuple(
        (
            jnp.concatenate([member[:, :head_dim] * factor, member[:, head_dim:]], axis=1)
            for member in finished[1:]
        )
    )
    return (out_rows, query_grad, kv_grads)


def body(queries, key_rows, values, out_grad, span_order):
    row_count = queries.shape[0]
    grp_count = lax.axis_size("grp")
    blk_count = lax.axis_size("blk")
    grp_idx = lax.axis_index("grp")
    blk_idx = lax.axis_index("blk")
    paired = jnp.concatenate([key_rows, values], axis=1)
    from_lower = from_behind(paired, "blk", 1)
    from_upper = from_behind(paired, "blk", -1)
    nearby = [(blk_idx + blk_count - 1) % blk_count, blk_idx, (blk_idx + 1) % blk_count]
    every_grp = jnp.arange(grp_count, dtype=jnp.int32)
    own_grp = jnp.reshape(grp_idx, (1,))
    gathered = (
        lax.all_gather(from_lower, "grp", axis=0, tiled=True),
        lax.all_gather(paired, "grp", axis=0, tiled=True),
        lax.all_gather(from_upper, "grp", axis=0, tiled=True),
    )
    query_pos = positions(span_order, own_grp, blk_idx, row_count, grp_count, blk_count)
    key_pos_sets = [
        positions(span_order, every_grp, neighbor, row_count, grp_count, blk_count)
        for neighbor in nearby
    ]
    out_own, query_own, grads_wide = attend(
        queries,
        out_grad,
        query_pos,
        [gathered[0], gathered[1], gathered[2]],
        key_pos_sets,
        lambda blended, totals: (blended, totals),
    )
    kv_grads = (
        lax.psum_scatter(
            grads_wide[0].astype(jnp.bfloat16), "grp", scatter_dimension=0, tiled=True
        ).astype(jnp.float32),
        lax.psum_scatter(
            grads_wide[1].astype(jnp.bfloat16), "grp", scatter_dimension=0, tiled=True
        ).astype(jnp.float32),
        lax.psum_scatter(
            grads_wide[2].astype(jnp.bfloat16), "grp", scatter_dimension=0, tiled=True
        ).astype(jnp.float32),
    )
    to_lower = from_behind(kv_grads[0].astype(jnp.bfloat16), "blk", -1).astype(jnp.float32)
    to_upper = from_behind(kv_grads[2].astype(jnp.bfloat16), "blk", 1).astype(jnp.float32)
    kv_total = kv_grads[1] + to_lower + to_upper
    return (
        out_own,
        query_own.astype(jnp.bfloat16),
        kv_total[:, :HEAD].astype(jnp.bfloat16),
        kv_total[:, HEAD:].astype(jnp.bfloat16),
    )


def solution(mesh):
    return jax.shard_map(
        body,
        mesh=mesh,
        in_specs=(
            P(("grp", "blk"), None),
            P(("grp", "blk"), None),
            P(("grp", "blk"), None),
            P(("grp", "blk"), None),
            P(),
        ),
        out_specs=(
            P(("grp", "blk"), None),
            P(("grp", "blk"), None),
            P(("grp", "blk"), None),
            P(("grp", "blk"), None),
        ),
        check_vma=False,
    )
```

profile of v0, /device:TPU:0, one launch (start us, length us, event | category | flops | bytes accessed | tf_op | source)
XLA Modules:
  0.0 199.8 jit_solution(18089019114384409987)
XLA Ops:
  8.0 4.6 %collective-permute-start.1 = (bf16[128,256]{1,0:T(8,128)(2,1)S(1)}, bf16[128,256]{1,0:T(8,128)(2,1)S(1)}, u32[]{:S(2)}, u32[]{:S(2)}) collective-permute-start(bf16[128,256]{1,0:T(8,128)(2,1)S(1)} %constant_dynamic-update-slice_fusion), channel_id=1, source_target_pairs={{1,0},{2,1},{3,2},{4,3},{5,4},{6,5},{7,6},{0,7},{9,8},{10,9},{11,1... | collective-permute-start | bytes 196616 | tf_op jit(solution)/shard_map/ppermute | solution.py:17
  12.6 9.1 %all_gather.10 = bf16[512,256]{1,0:T(8,128)(2,1)S(1)} all-gather(bf16[128,256]{1,0:T(8,128)(2,1)S(1)} %constant_dynamic-update-slice_fusion), channel_id=1, replica_groups=mesh['grp'=4,'blk'=8] {'grp'}, dimensions={0}, use_global_device_ids=true | all-gather | bytes 327680 | tf_op jit(solution)/shard_map/all_gather | solution.py:158
  25.0 0.9 copy-done
  26.0 0.9 copy.26
  26.8 1.3 multiply_add_fusion
  29.5 8.9 %all_gather.9 = bf16[512,256]{1,0:T(8,128)(2,1)S(1)} all-gather(bf16[128,256]{1,0:T(8,128)(2,1)S(1)} %collective-permute-done), channel_id=1, replica_groups=mesh['grp'=4,'blk'=8] {'grp'}, dimensions={0}, use_global_device_ids=true | all-gather | bytes 327680 | tf_op jit(solution)/shard_map/all_gather | solution.py:157
  38.4 8.1 %all_gather.11 = bf16[512,256]{1,0:T(8,128)(2,1)S(1)} all-gather(bf16[128,256]{1,0:T(8,128)(2,1)S(1)} %collective-permute-done.1), channel_id=1, replica_groups=mesh['grp'=4,'blk'=8] {'grp'}, dimensions={0}, use_global_device_ids=true | all-gather | bytes 327680 | tf_op jit(solution)/shard_map/all_gather | solution.py:159
  47.5 22.1 %while.38 = (s32[]{:T(128)}, f32[128,1024]{1,0:T(8,128)}, f32[128,8]{0,1:T(8,128)S(1)}, f32[128,8]{0,1:T(8,128)S(1)}, bf16[128,1024]{1,0:T(8,128)(2,1)S(1)}, /*i...) while((s32[]{:T(128)}, f32[128,1024]{1,0:T(8,128)}, ...), condition=%wide.region_10.11_spmd.clone, body=%wide.region_3.10_spmd.clone.sunk | while | flops 103056896 | bytes 3611951 | solution.py:85
  49.3 0.9 fusion.221
  52.1 0.9 fusion.221
  54.8 0.9 fusion.221
  57.6 0.9 fusion.221
  60.4 0.9 fusion.221
  63.1 0.9 fusion.221
  65.9 0.9 fusion.221
  68.7 0.9 fusion.221
  69.6 2.0 copy.24
  71.6 1.2 fusion.109
  72.9 1.3 multiply_reduce_fusion
  75.1 38.2 %while.39 = (s32[]{:T(128)}, f32[128,1024]{1,0:T(8,128)}, f32[512,256]{0,1:T(8,128)S(1)}, f32[512,256]{0,1:T(8,128)S(1)}, f32[512,256]{0,1:T(8,128)S(1)}, /*inde...) while((s32[]{:T(128)}, f32[128,1024]{1,0:T(8,128)}, ...), condition=%wide.region_13.14_spmd.clone, body=%wide.region_12.13_spmd.clone.sunk | while | flops 254838400 | bytes 11753354 | solution.py:133
  116.4 20.6 %reduce-scatter.8.cloned.1.call-done = bf16[128,256]{1,0:T(8,128)(2,1)} async-done(((bf16[512,256]{1,0:T(8,128)(2,1)}), bf16[128,256]{1,0:T(8,128)(2,1)}) %reduce-scatter.8.cloned.1.call-update) | async-done | bytes 65552 | tf_op jit(solution)/shard_map/reduce_scatter | solution.py:181
  137.0 27.7 %reduce-scatter.6.cloned.1.call-done = bf16[128,256]{1,0:T(8,128)(2,1)} async-done(((bf16[512,256]{1,0:T(8,128)(2,1)}), bf16[128,256]{1,0:T(8,128)(2,1)}) %reduce-scatter.6.cloned.1.call-update) | async-done | bytes 65552 | tf_op jit(solution)/shard_map/reduce_scatter | solution.py:175
  164.6 2.2 %collective-permute-start.2 = (bf16[128,256]{1,0:T(8,128)(2,1)}, bf16[128,256]{1,0:T(8,128)(2,1)S(1)}, u32[]{:S(2)}, u32[]{:S(2)}) collective-permute-start(bf16[128,256]{1,0:T(8,128)(2,1)} %reduce-scatter.6.cloned.1.call-done), channel_id=1, source_target_pairs={{1,0},{2,1},{3,2},{4,3},{5,4},{6,5},{7,6},{0,7},{9,8},{10,9},{11,1... | collective-permute-start | bytes 196616 | tf_op jit(solution)/shard_map/ppermute | solution.py:17
  168.4 23.4 %reduce-scatter.4.cloned.1.call-done = bf16[128,256]{1,0:T(8,128)(2,1)} async-done(((bf16[512,256]{1,0:T(8,128)(2,1)}), bf16[128,256]{1,0:T(8,128)(2,1)}) %reduce-scatter.4.cloned.1.call-update) | async-done | bytes 65552 | tf_op jit(solution)/shard_map/reduce_scatter | solution.py:178
  (350 shorter events, 62.8 us)
Async XLA Ops:
  7.2 0.8 copy-start.3
  7.2 129.8 %reduce-scatter.8.cloned.1.call-start = ((), (), s32[]{:S(2)}) async-start(), calls=%async_computation.5 | async-start | bytes 327680 | tf_op jit(solution)/shard_map/reduce_scatter | solution.py:181
  8.0 30.4 %collective-permute-start.1 = (bf16[128,256]{1,0:T(8,128)(2,1)S(1)}, bf16[128,256]{1,0:T(8,128)(2,1)S(1)}, u32[]{:S(2)}, u32[]{:S(2)}) collective-permute-start(bf16[128,256]{1,0:T(8,128)(2,1)S(1)} %constant_dynamic-update-slice_fusion), channel_id=1, source_target_pairs={{1,0},{2,1},{3,2},{4,3},{5,4},{6,5},{7,6},{0,7},{9,8},{10,9},{11,1... | collective-permute-start | bytes 196616 | tf_op jit(solution)/shard_map/ppermute | solution.py:17
  12.6 16.9 %collective-permute-start = (bf16[128,256]{1,0:T(8,128)(2,1)S(1)}, bf16[128,256]{1,0:T(8,128)(2,1)S(1)}, u32[]{:S(2)}, u32[]{:S(2)}) collective-permute-start(bf16[128,256]{1,0:T(8,128)(2,1)S(1)} %constant_dynamic-update-slice_fusion), channel_id=1, source_target_pairs={{7,0},{0,1},{1,2},{2,3},{3,4},{4,5},{5,6},{6,7},{15,8},{8,9},{9,10... | collective-permute-start | bytes 196616 | tf_op jit(solution)/shard_map/ppermute | solution.py:17
  21.7 0.7 copy-start.4
  25.0 1.0 copy-start
  46.5 1.0 copy-start.1
  114.2 50.4 %reduce-scatter.6.cloned.1.call-start = ((), (), s32[]{:S(2)}) async-start(), calls=%async_computation.4 | async-start | bytes 327680 | tf_op jit(solution)/shard_map/reduce_scatter | solution.py:175
  115.3 76.5 %reduce-scatter.4.cloned.1.call-start = ((), (), s32[]{:S(2)}) async-start(), calls=%async_computation.3 | async-start | bytes 327680 | tf_op jit(solution)/shard_map/reduce_scatter | solution.py:178
  115.6 51.3 %copy-start.2 = (f32[128,1024]{1,0:T(8,128)S(1)}, f32[128,1024]{1,0:T(8,128)}, u32[]{:S(2)}) copy-start(f32[128,1024]{1,0:T(8,128)} %get-tuple-element.575) | copy-start | bytes 1572868
  136.9 54.8 %collective-permute-start.3 = (bf16[128,256]{1,0:T(8,128)(2,1)}, bf16[128,256]{1,0:T(8,128)(2,1)S(1)}, u32[]{:S(2)}, u32[]{:S(2)}) collective-permute-start(bf16[128,256]{1,0:T(8,128)(2,1)} %reduce-scatter.8.cloned.1.call-done), channel_id=1, source_target_pairs={{7,0},{0,1},{1,2},{2,3},{3,4},{4,5},{5,6},{6,7},{15,8},{8,9},{9,10... | collective-permute-start | bytes 196616 | tf_op jit(solution)/shard_map/ppermute | solution.py:17
  164.6 27.1 %collective-permute-start.2 = (bf16[128,256]{1,0:T(8,128)(2,1)}, bf16[128,256]{1,0:T(8,128)(2,1)S(1)}, u32[]{:S(2)}, u32[]{:S(2)}) collective-permute-start(bf16[128,256]{1,0:T(8,128)(2,1)} %reduce-scatter.6.cloned.1.call-done), channel_id=1, source_target_pairs={{1,0},{2,1},{3,2},{4,3},{5,4},{6,5},{7,6},{0,7},{9,8},{10,9},{11,1... | collective-permute-start | bytes 196616 | tf_op jit(solution)/shard_map/ppermute | solution.py:17
Sparse Core Ops, SparseCore 0:
  114.3 22.5 reduce-scatter.7
  140.3 24.3 reduce-scatter.5
  167.4 24.3 reduce-scatter.3
where the time goes:
time: 200 us
  waiting for transfers between devices  71.7 us (36%)
  matrix products  48.4 us (24%)
  blocking collectives  26 us (13%)
  other arithmetic  18.9 us (9%)
  between operations  16.6 us (8%)
  local copies, waits for them, and re-layouts  9.97 us (5%)
  starting transfers between devices  6.93 us (3%)
    reduce_scatter x1, waiting for transfers between devices, body(): lax.psum_scatter(grads_wide[0].astype(jnp.bfloat16), 'grp', scatter_dimen...  27.7 us
    reduce_scatter x1, waiting for transfers between devices, body(): lax.psum_scatter(grads_wide[1].astype(jnp.bfloat16), 'grp', scatter_dimen...  23.4 us
    reduce_scatter x1, waiting for transfers between devices, body(): lax.psum_scatter(grads_wide[2].astype(jnp.bfloat16), 'grp', scatter_dimen...  20.6 us
    dot_general x48, matrix products, masked_scores(): jnp.einsum('qd,kd->qk', query_head, key_head, preferred_element_type=jnp....  12.2 us
    dot_general x24, matrix products, forward_step(): jnp.dot(weights.astype(jnp.bfloat16), value_list[member], preferred_eleme...  11 us
    dot_general x24, matrix products, backward_step(): jnp.dot(score_grad, key_list[member], preferred_element_type=jnp.float32)  9.38 us
    all_gather x1, blocking collectives, body(): lax.all_gather(paired, 'grp', axis=0, tiled=True)  9.08 us
    all_gather x1, blocking collectives, body(): lax.all_gather(from_lower, 'grp', axis=0, tiled=True)  8.87 us
  transfers between devices with their start and end apart: 7, of which 3 were waited for; matrix products, arithmetic and copies ran while one was open for 4% of the time, Pallas kernels for 0%

commit v1 on v0

v1 whole, which is shorter than its diff:
```python
import functools
import math

import jax
import jax.numpy as jnp
from jax import lax
from jax.experimental import pallas as pl
from jax.experimental.pallas import tpu as pltpu
from jax.sharding import PartitionSpec as P

HEAD = 128
NEG_FILL = -1e30
F32 = jnp.float32
BF16 = jnp.bfloat16
NT = (((1,), (1,)), ((), ()))


def dot(a, b):
    return jnp.dot(a, b, preferred_element_type=F32)


def dot_nt(a, b):
    return lax.dot_general(a, b, NT, preferred_element_type=F32)


def kernel(
    half, blk_count, span_ref, q_ref, go_ref, so, eo, sm, em, sf, ef,
    out_ref, gq_ref, gso, geo, gsm, gem, gsf, gef,
    qs, gos, got, w_ref, m_ref, m_run, l_run, o_run, gq_run, delta,
):
    rows, width = q_ref.shape
    heads = width // HEAD
    pair = 2 * rows
    pairs = heads // 2
    unit = so.shape[0]
    chunk = min(unit, 2 * rows)
    per_unit = unit // chunk
    factor = 1.0 / math.sqrt(HEAD)
    c2 = factor * math.log2(math.e)
    grp = lax.axis_index("grp")
    blk = lax.axis_index("blk")
    late = grp >= half
    idx = lax.rem(grp, half)
    even = lax.rem(blk, 2) == 0
    below = lax.rem(blk + blk_count - 1, blk_count)
    above = lax.rem(blk + 1, blk_count)
    mine = span_ref[blk]
    mate = span_ref[jnp.where(even, above, below)]
    off = span_ref[jnp.where(even, below, above)]
    see_m = late == (mate > mine)
    see_f = late == (off > mine)
    units = [
        (so, gso, None), (eo, geo, late), (sm, gsm, see_m), (em, gem, late), (sf, gsf, see_f), (ef, gef, late),
    ]

    for h in range(heads):
        qs[h * rows : (h + 1) * rows, :] = q_ref[:, h * HEAD : (h + 1) * HEAD]
        gh = go_ref[:, h * HEAD : (h + 1) * HEAD]
        gos[h * rows : (h + 1) * rows, :] = gh
        got[:, h * rows : (h + 1) * rows] = gh.T
    m_run[...] = jnp.full_like(m_run, NEG_FILL)
    l_run[...] = jnp.zeros_like(l_run)
    o_run[...] = jnp.zeros_like(o_run)
    gq_run[...] = jnp.zeros_like(gq_run)

    def forward(kv, slot, r0, mask):
        k = kv[r0 : r0 + chunk, :HEAD]
        vt = kv[r0 : r0 + chunk, HEAD:].T
        for p in range(pairs):
            cols = slice(p * pair, (p + 1) * pair)
            s = dot_nt(k, qs[cols, :]) * c2
            if mask is not None:
                s = jnp.where(mask, s, NEG_FILL)
            m_old = m_run[:, cols]
            m_new = jnp.maximum(m_old, jnp.max(s, axis=0, keepdims=True))
            w = jnp.exp2(s - m_new)
            if mask is not None:
                w = jnp.where(mask, w, 0.0)
            alpha = jnp.exp2(m_old - m_new)
            l_run[:, cols] = l_run[:, cols] * alpha + jnp.sum(w, axis=0, keepdims=True)
            w16 = w.astype(BF16)
            w_ref[slot, :, cols] = w16
            o_run[:, cols] = o_run[:, cols] * alpha + dot(vt, w16)
            m_run[:, cols] = m_new
            m_ref[slot, :, cols] = m_new

    def backward(kv, gkv, slot, r0):
        k = kv[r0 : r0 + chunk, :HEAD]
        kt = k.T
        v = kv[r0 : r0 + chunk, HEAD:]
        gk = jnp.zeros((chunk, HEAD), F32)
        gv = jnp.zeros((chunk, HEAD), F32)
        for p in range(pairs):
            cols = slice(p * pair, (p + 1) * pair)
            scale = jnp.exp2(m_ref[slot, :, cols] - m_run[:, cols]) * l_run[:, cols]
            prob = w_ref[slot, :, cols].astype(F32) * scale
            dp = dot_nt(v, gos[cols, :])
            ds = (prob * (dp - delta[:, cols])).astype(BF16)
            gv = gv + dot(prob.astype(BF16), gos[cols, :])
            gk = gk + dot(ds, qs[cols, :])
            gq_run[:, cols] = gq_run[:, cols] + dot(kt, ds)
        gkv[r0 : r0 + chunk, :HEAD] = (gk * factor).astype(BF16)
        gkv[r0 : r0 + chunk, HEAD:] = gv.astype(BF16)

    for i, (kv, gkv, see) in enumerate(units):
        for j in range(per_unit):
            slot, r0 = i * per_unit + j, j * chunk
            if see is None:
                row = lax.broadcasted_iota(jnp.int32, (chunk, pair), 0) + r0
                col = lax.broadcasted_iota(jnp.int32, (chunk, pair), 1)
                col = jnp.where(col >= rows, col - rows, col)
                mask = (row <= col) | ((row >= rows) & (row < (idx + 1) * rows))
                forward(kv, slot, r0, mask)
            else:
                pl.when(see)(functools.partial(forward, kv, slot, r0, None))

    for p in range(pairs):
        cols = slice(p * pair, (p + 1) * pair)
        inv = 1.0 / l_run[:, cols]
        l_run[:, cols] = inv
        o16 = (o_run[:, cols] * inv).astype(BF16)
        delta[:, cols] = jnp.sum(o16.astype(F32) * got[:, cols].astype(F32), axis=0, keepdims=True)
        for t in range(2):
            h = 2 * p + t
            out_ref[:, h * HEAD : (h + 1) * HEAD] = o16[:, t * rows : (t + 1) * rows].T

    for i, (kv, gkv, see) in enumerate(units):
        for j in range(per_unit):
            slot, r0 = i * per_unit + j, j * chunk
            if see is None:
                backward(kv, gkv, slot, r0)
            else:
                pl.when(see)(functools.partial(backward, kv, gkv, slot, r0))

                @pl.when(jnp.logical_not(see))
                def _():
                    gkv[r0 : r0 + chunk, :] = jnp.zeros((chunk, 2 * HEAD), BF16)

    for h in range(heads):
        g16 = (gq_run[:, h * rows : (h + 1) * rows] * factor).astype(BF16)
        gq_ref[:, h * HEAD : (h + 1) * HEAD] = g16.T


def attend(queries, grads, span_order, half, blk_count, units):
    rows, width = queries.shape
    unit = units[0].shape[0]
    chunk = min(unit, 2 * rows)
    slots = 6 * (unit // chunk)
    big = width // HEAD * rows
    vmem = pl.BlockSpec(memory_space=pltpu.VMEM)
    smem = pl.BlockSpec(memory_space=pltpu.SMEM)
    like = jax.ShapeDtypeStruct
    return pl.pallas_call(
        functools.partial(kernel, half, blk_count),
        out_shape=[like((rows, width), BF16)] * 2 + [like((unit, 2 * HEAD), BF16)] * 6,
        in_specs=[smem] + [vmem] * 8,
        out_specs=[vmem] * 8,
        scratch_shapes=[
            pltpu.VMEM((big, HEAD), BF16),
            pltpu.VMEM((big, HEAD), BF16),
            pltpu.VMEM((HEAD, big), BF16),
            pltpu.VMEM((slots, chunk, big), BF16),
            pltpu.VMEM((slots, 1, big), F32),
            pltpu.VMEM((1, big), F32),
            pltpu.VMEM((1, big), F32),
            pltpu.VMEM((HEAD, big), F32),
            pltpu.VMEM((HEAD, big), F32),
            pltpu.VMEM((1, big), F32),
        ],
        compiler_params=pltpu.CompilerParams(vmem_limit_bytes=40 << 20),
        name="attend",
    )(span_order, queries, grads, *units)


def body(queries, key_rows, values, out_grad, span_order):
    rows = queries.shape[0]
    grp_count = lax.axis_size("grp")
    blk_count = lax.axis_size("blk")
    half = grp_count // 2

    def send(block, grp_to, blk_to):
        route = []
        for g in range(grp_count):
            for b in range(blk_count):
                to = grp_to(g)
                if to is not None:
                    route.append((g * blk_count + b, to * blk_count + blk_to(b) % blk_count))
        return lax.ppermute(block, ("grp", "blk"), route)

    same = lambda i: i
    on_chip = lambda block: send(block, same, lambda b: b ^ 1)
    off_chip = lambda block: send(block, same, lambda b: b + 1 if b % 2 else b - 1)
    ring_up = lambda block: send(block, lambda g: g // half * half + (g + 1) % half, same)
    ring_down = lambda block: send(block, lambda g: g // half * half + (g - 1) % half, same)
    to_late = lambda block: send(block, lambda g: g + half if g < half else None, same)
    to_early = lambda block: send(block, lambda g: g - half if g >= half else None, same)

    own = jnp.concatenate([key_rows, values], axis=1)
    off = off_chip(own)
    parts = [jnp.concatenate([own, off], axis=0)]
    for _ in range(half - 1):
        parts.append(ring_up(parts[-1]))
    near = jnp.concatenate([p[:rows] for p in parts] + [p[rows:] for p in parts], axis=0)
    far = to_late(near)
    unit = half * rows
    so, sf, eo, ef = near[:unit], near[unit:], far[:unit], far[unit:]
    mate = on_chip(jnp.concatenate([so, eo], axis=0))
    sm, em = mate[:unit], mate[unit:]

    out, gq, gso, geo, gsm, gem, gsf, gef = attend(
        queries, out_grad, span_order, half, blk_count, [so, eo, sm, em, sf, ef]
    )

    add = lambda a, b: (a.astype(F32) + b.astype(F32)).astype(BF16)
    mate = on_chip(jnp.concatenate([gsm, gem], axis=0))
    gso, geo = add(gso, mate[:unit]), add(geo, mate[unit:])
    back = to_early(jnp.concatenate([geo, gef], axis=0))
    gso, gsf = add(gso, back[:unit]), add(gsf, back[unit:])
    slots = [
        jnp.concatenate([gso[s * rows : (s + 1) * rows], gsf[s * rows : (s + 1) * rows]], axis=0)
        for s in range(half)
    ]
    total = slots[-1]
    for s in range(half - 2, -1, -1):
        total = add(ring_down(total), slots[s])
    final = add(total[:rows], off_chip(total[rows:]))
    return (out, gq, final[:, :HEAD], final[:, HEAD:])


def solution(mesh):
    spec = P(("grp", "blk"), None)
    return jax.shard_map(
        body,
        mesh=mesh,
        in_specs=(spec, spec, spec, spec, P()),
        out_specs=(spec, spec, spec, spec),
        check_vma=False,
    )
```

time: 200 us -> 62.2 us (0.31)
  matrix products: 48.4 us -> 0 us
  waiting for transfers between devices: 71.7 us -> 38.6 us
  blocking collectives: 26 us -> 0 us
  other arithmetic: 18.9 us -> 0.28 us
  between operations: 16.6 us -> 0.82 us
  local copies, waits for them, and re-layouts: 9.97 us -> 2.14 us
  starting transfers between devices: 6.93 us -> 14.7 us
  Pallas kernels: 0 us -> 6.13 us
    reduce_scatter x3 -> x0, waiting for transfers between devices: 71.6 us -> none  [the longest x1 27.7 us: body(): lax.psum_scatter(grads_wide[0].astype(jnp.bfloat16), 'grp', scatter_dimen...]
    dot_general x168 -> x0, matrix products: 48.4 us -> none  [the longest x48 12.2 us: masked_scores(): jnp.einsum('qd,kd->qk', query_head, key_head, preferred_element_type=jnp....]
    ppermute x4 -> x8, waiting for transfers between devices: 0.01 us -> 38.6 us  [send(): return lax.ppermute(block, ('grp', 'blk'), route)]
    all_gather x3 -> x0, blocking collectives: 26 us -> none  [the longest x1 9.08 us: body(): lax.all_gather(paired, 'grp', axis=0, tiled=True)]
    ppermute x4 -> x8, starting transfers between devices: 6.81 us -> 14.7 us  [send(): return lax.ppermute(block, ('grp', 'blk'), route)]
    add x26 -> x0, other arithmetic: 6.42 us -> none  [the longest x16 4.43 us: backward_step(): running[1 + member] + jnp.concatenate([key_grad, value_grad], axis=1)]
    pallas_call x0 -> x1, Pallas kernels: none -> 6.13 us  [attend(): pl.pallas_call(functools.partial(kernel, half, blk_count), out_shape=[lik...]
    unnamed x15 -> x9, local copies, waits for them, and re-layouts: 6.05 us -> 1.42 us
  transfers between devices with their start and end apart: 7 -> 8, of which waited for: 3 -> 8; matrix products, arithmetic and copies ran while one was open for 4% -> 0% of each run, Pallas kernels for 0% -> 0%
where the time goes in v1:
time: 62.2 us; the launch traced here: 62.6 us
  waiting for transfers between devices  38.6 us (62%)
  starting transfers between devices  14.7 us (24%)
  Pallas kernels  6.13 us (10%)
  local copies, waits for them, and re-layouts  2.14 us (3%)
  between operations  0.82 us (1%)
    ppermute x8, waiting for transfers between devices, send(): return lax.ppermute(block, ('grp', 'blk'), route)  38.6 us
    ppermute x8, starting transfers between devices, send(): return lax.ppermute(block, ('grp', 'blk'), route)  14.7 us
    pallas_call x1, Pallas kernels, attend(): pl.pallas_call(functools.partial(kernel, half, blk_count), out_shape=[lik...  6.13 us
    unnamed x9, local copies, waits for them, and re-layouts  1.42 us
  transfers between devices with their start and end apart: 8, of which 8 were waited for; matrix products, arithmetic and copies ran while one was open for 0% of the time, Pallas kernels for 0%

profile of v1, /device:TPU:0, one launch (start us, length us, event | category | flops | bytes accessed | tf_op | source)
XLA Modules:
  0.0 62.6 jit_solution(4520740168938531126)
XLA Ops:
  0.6 0.8 %constant_dynamic-update-slice_fusion.1 = bf16[128,256]{1,0:T(8,128)(2,1)S(1)} fusion(bf16[128,128]{1,0:T(8,128)(2,1)} %param.6), kind=kLoop, calls=%fused_computation.16 | loop fusion | bytes 65536
  1.4 4.6 %collective-permute-start = (bf16[128,256]{1,0:T(8,128)(2,1)S(1)}, bf16[128,256]{1,0:T(8,128)(2,1)S(1)}, u32[]{:S(2)}, u32[]{:S(2)}) collective-permute-start(bf16[128,256]{1,0:T(8,128)(2,1)S(1)} %constant_dynamic-update-slice_fusion), channel_id=1, source_target_pairs={{0,7},{1,2},{2,1},{3,4},{4,3},{5,6},{6,5},{7,0},{8,15},{9,10},{10,... | collective-permute-start | bytes 196616 | tf_op jit(solution)/shard_map/ppermute | solution.py:188
  6.0 2.1 %collective-permute-done = bf16[128,256]{1,0:T(8,128)(2,1)S(1)} collective-permute-done((bf16[128,256]{1,0:T(8,128)(2,1)S(1)}, bf16[128,256]{1,0:T(8,128)(2,1)S(1)}, u32[]{:S(2)}, u32[]{:S(2)}) %collective-permute-start) | collective-permute-done | bytes 65568 | tf_op jit(solution)/shard_map/ppermute | solution.py:188
  8.1 2.3 %collective-permute-start.1 = (bf16[256,256]{1,0:T(8,128)(2,1)S(1)}, bf16[256,256]{1,0:T(8,128)(2,1)S(1)}, u32[]{:S(2)}, u32[]{:S(2)}) collective-permute-start(bf16[256,256]{1,0:T(8,128)(2,1)S(1)} %pad_maximum_fusion.5), channel_id=1, source_target_pairs={{0,8},{1,9},{2,10},{3,11},{4,12},{5,13},{6,14},{7,15},{8,0},{9,1},... | collective-permute-start | bytes 393224 | tf_op jit(solution)/shard_map/ppermute | solution.py:188
  10.4 2.9 %collective-permute-done.1 = bf16[256,256]{1,0:T(8,128)(2,1)S(1)} collective-permute-done((bf16[256,256]{1,0:T(8,128)(2,1)S(1)}, bf16[256,256]{1,0:T(8,128)(2,1)S(1)}, u32[]{:S(2)}, u32[]{:S(2)}) %collective-permute-start.1) | collective-permute-done | bytes 131104 | tf_op jit(solution)/shard_map/ppermute | solution.py:188
  13.4 4.0 %collective-permute-start.2 = (bf16[512,256]{1,0:T(8,128)(2,1)S(1)}, bf16[512,256]{1,0:T(8,128)(2,1)S(1)}, u32[]{:S(2)}, u32[]{:S(2)}) collective-permute-start(bf16[512,256]{1,0:T(8,128)(2,1)S(1)} %pad_maximum_fusion), channel_id=1, source_target_pairs={{0,16},{1,17},{2,18},{3,19},{4,20},{5,21},{6,22},{7,23},{8,24},{9,... | collective-permute-start | bytes 786440 | tf_op jit(solution)/shard_map/ppermute | solution.py:188
  17.3 3.9 %collective-permute-done.2 = bf16[512,256]{1,0:T(8,128)(2,1)S(1)} collective-permute-done((bf16[512,256]{1,0:T(8,128)(2,1)S(1)}, bf16[512,256]{1,0:T(8,128)(2,1)S(1)}, u32[]{:S(2)}, u32[]{:S(2)}) %collective-permute-start.2) | collective-permute-done | bytes 262176 | tf_op jit(solution)/shard_map/ppermute | solution.py:188
  21.2 0.1 collective-permute-start.3
  21.4 0.0 copy-start
  21.4 0.0 copy-start.1
  21.4 1.5 %collective-permute-done.3 = bf16[512,256]{1,0:T(8,128)(2,1)S(1)} collective-permute-done((bf16[512,256]{1,0:T(8,128)(2,1)S(1)}, bf16[512,256]{1,0:T(8,128)(2,1)S(1)}, u32[]{:S(2)}, u32[]{:S(2)}) %collective-permute-start.3) | collective-permute-done | bytes 262176 | tf_op jit(solution)/shard_map/ppermute | solution.py:188
  22.9 0.0 copy-start.2
  22.9 0.6 %copy-done.2 = s32[8]{0:T(128)S(1)} copy-done((s32[8]{0:T(128)S(1)}, s32[8]{0:T(128)}, u32[]{:S(2)}) %copy-start.2) | copy-done | bytes 56
  23.5 6.1 %attend.1 = (bf16[128,1024]{1,0:T(8,128)(2,1)}, bf16[128,1024]{1,0:T(8,128)(2,1)}, bf16[256,256]{1,0:T(8,128)(2,1)S(1)}, bf16[256,256]{1,0:T(8,128)(2,1)S(1)}, b...) custom-call(s32[8]{0:T(128)S(1)} %copy-done.2, ...), custom_call_target="tpu_custom_call" | custom-call | tf_op jit(solution)/shard_map/attend/pallas_call | solution.py:153
  29.7 0.1 collective-permute-start.4
  29.8 1.5 %collective-permute-done.4 = bf16[512,256]{1,0:T(8,128)(2,1)S(1)} collective-permute-done((bf16[512,256]{1,0:T(8,128)(2,1)S(1)}, bf16[512,256]{1,0:T(8,128)(2,1)S(1)}, u32[]{:S(2)}, u32[]{:S(2)}) %collective-permute-start.4) | collective-permute-done | bytes 262176 | tf_op jit(solution)/shard_map/ppermute | solution.py:188
  31.3 1.3 %collective-permute-start.5 = (bf16[512,256]{1,0:T(8,128)(2,1)S(1)}, bf16[512,256]{1,0:T(8,128)(2,1)S(1)}, u32[]{:S(2)}, u32[]{:S(2)}) collective-permute-start(bf16[512,256]{1,0:T(8,128)(2,1)S(1)} %pad_maximum_fusion.4), channel_id=1, source_target_pairs={{16,0},{17,1},{18,2},{19,3},{20,4},{21,5},{22,6},{23,7},{24,8},{25... | collective-permute-start | bytes 786440 | tf_op jit(solution)/shard_map/ppermute | solution.py:188
  32.6 18.3 %collective-permute-done.5 = bf16[512,256]{1,0:T(8,128)(2,1)S(1)} collective-permute-done((bf16[512,256]{1,0:T(8,128)(2,1)S(1)}, bf16[512,256]{1,0:T(8,128)(2,1)S(1)}, u32[]{:S(2)}, u32[]{:S(2)}) %collective-permute-start.5) | collective-permute-done | bytes 262176 | tf_op jit(solution)/shard_map/ppermute | solution.py:188
  50.9 0.1 add_convert_fusion.2
  51.1 1.6 %collective-permute-start.6 = (bf16[256,256]{1,0:T(8,128)(2,1)S(1)}, bf16[256,256]{1,0:T(8,128)(2,1)S(1)}, u32[]{:S(2)}, u32[]{:S(2)}) collective-permute-start(bf16[256,256]{1,0:T(8,128)(2,1)S(1)} %pad_maximum_fusion.8), channel_id=1, source_target_pairs={{0,8},{1,9},{2,10},{3,11},{4,12},{5,13},{6,14},{7,15},{8,0},{9,1},... | collective-permute-start | bytes 393224 | tf_op jit(solution)/shard_map/ppermute | solution.py:188
  52.6 3.7 %collective-permute-done.6 = bf16[256,256]{1,0:T(8,128)(2,1)S(1)} collective-permute-done((bf16[256,256]{1,0:T(8,128)(2,1)S(1)}, bf16[256,256]{1,0:T(8,128)(2,1)S(1)}, u32[]{:S(2)}, u32[]{:S(2)}) %collective-permute-start.6) | collective-permute-done | bytes 131104 | tf_op jit(solution)/shard_map/ppermute | solution.py:188
  56.4 0.8 %collective-permute-start.7 = (bf16[128,256]{1,0:T(8,128)(2,1)S(1)}, bf16[128,256]{1,0:T(8,128)(2,1)S(1)}, u32[]{:S(2)}, u32[]{:S(2)}) collective-permute-start(bf16[128,256]{1,0:T(8,128)(2,1)S(1)} %slice.91), channel_id=1, source_target_pairs={{0,7},{1,2},{2,1},{3,4},{4,3},{5,6},{6,5},{7,0},{8,15},{9,10},{10,... | collective-permute-start | bytes 196616 | tf_op jit(solution)/shard_map/ppermute | solution.py:188
  57.2 4.7 %collective-permute-done.7 = bf16[128,256]{1,0:T(8,128)(2,1)S(1)} collective-permute-done((bf16[128,256]{1,0:T(8,128)(2,1)S(1)}, bf16[128,256]{1,0:T(8,128)(2,1)S(1)}, u32[]{:S(2)}, u32[]{:S(2)}) %collective-permute-start.7) | collective-permute-done | bytes 65568 | tf_op jit(solution)/shard_map/ppermute | solution.py:188
  62.0 0.6 %fusion.5 = (bf16[128,128]{1,0:T(8,128)(2,1)}, bf16[128,128]{1,0:T(8,128)(2,1)}) fusion(bf16[128,256]{1,0:T(8,128)(2,1)S(1)} %add_convert_fusion.5), kind=kLoop, calls=%fused_computation.22 | loop fusion | bytes 131072 | tf_op jit(solution)/shard_map/slice | solution.py:227
  (21 shorter events, 0.3 us)
Async XLA Ops:
  0.6 0.8 %copy-start.3 = (bf16[128,128]{1,0:T(8,128)(2,1)S(1)}, bf16[128,128]{1,0:T(8,128)(2,1)}, u32[]{:S(2)}) copy-start(bf16[128,128]{1,0:T(8,128)(2,1)} %param.7) | copy-start | bytes 98308
  1.4 6.6 %collective-permute-start = (bf16[128,256]{1,0:T(8,128)(2,1)S(1)}, bf16[128,256]{1,0:T(8,128)(2,1)S(1)}, u32[]{:S(2)}, u32[]{:S(2)}) collective-permute-start(bf16[128,256]{1,0:T(8,128)(2,1)S(1)} %constant_dynamic-update-slice_fusion), channel_id=1, source_target_pairs={{0,7},{1,2},{2,1},{3,4},{4,3},{5,6},{6,5},{7,0},{8,15},{9,10},{10,... | collective-permute-start | bytes 196616 | tf_op jit(solution)/shard_map/ppermute | solution.py:188
  8.1 5.2 %collective-permute-start.1 = (bf16[256,256]{1,0:T(8,128)(2,1)S(1)}, bf16[256,256]{1,0:T(8,128)(2,1)S(1)}, u32[]{:S(2)}, u32[]{:S(2)}) collective-permute-start(bf16[256,256]{1,0:T(8,128)(2,1)S(1)} %pad_maximum_fusion.5), channel_id=1, source_target_pairs={{0,8},{1,9},{2,10},{3,11},{4,12},{5,13},{6,14},{7,15},{8,0},{9,1},... | collective-permute-start | bytes 393224 | tf_op jit(solution)/shard_map/ppermute | solution.py:188
  13.4 7.8 %collective-permute-start.2 = (bf16[512,256]{1,0:T(8,128)(2,1)S(1)}, bf16[512,256]{1,0:T(8,128)(2,1)S(1)}, u32[]{:S(2)}, u32[]{:S(2)}) collective-permute-start(bf16[512,256]{1,0:T(8,128)(2,1)S(1)} %pad_maximum_fusion), channel_id=1, source_target_pairs={{0,16},{1,17},{2,18},{3,19},{4,20},{5,21},{6,22},{7,23},{8,24},{9,... | collective-permute-start | bytes 786440 | tf_op jit(solution)/shard_map/ppermute | solution.py:188
  21.2 1.6 %collective-permute-start.3 = (bf16[512,256]{1,0:T(8,128)(2,1)S(1)}, bf16[512,256]{1,0:T(8,128)(2,1)S(1)}, u32[]{:S(2)}, u32[]{:S(2)}) collective-permute-start(bf16[512,256]{1,0:T(8,128)(2,1)S(1)} %pad_maximum_fusion.2), channel_id=1, source_target_pairs={{0,1},{1,0},{2,3},{3,2},{4,5},{5,4},{6,7},{7,6},{8,9},{9,8},{10,11... | collective-permute-start | bytes 786440 | tf_op jit(solution)/shard_map/ppermute | solution.py:188
  21.4 1.5 %copy-start = (bf16[128,1024]{1,0:T(8,128)(2,1)S(1)}, bf16[128,1024]{1,0:T(8,128)(2,1)}, u32[]{:S(2)}) copy-start(bf16[128,1024]{1,0:T(8,128)(2,1)} %q_ref.1) | copy-start | bytes 786436
  21.4 1.5 %copy-start.1 = (bf16[128,1024]{1,0:T(8,128)(2,1)S(1)}, bf16[128,1024]{1,0:T(8,128)(2,1)}, u32[]{:S(2)}) copy-start(bf16[128,1024]{1,0:T(8,128)(2,1)} %go_ref.1) | copy-start | bytes 786436
  22.9 0.7 %copy-start.2 = (s32[8]{0:T(128)S(1)}, s32[8]{0:T(128)}, u32[]{:S(2)}) copy-start(s32[8]{0:T(128)} %span_ref.1) | copy-start | bytes 100
  29.7 1.6 %collective-permute-start.4 = (bf16[512,256]{1,0:T(8,128)(2,1)S(1)}, bf16[512,256]{1,0:T(8,128)(2,1)S(1)}, u32[]{:S(2)}, u32[]{:S(2)}) collective-permute-start(bf16[512,256]{1,0:T(8,128)(2,1)S(1)} %pad_maximum_fusion.3), channel_id=1, source_target_pairs={{0,1},{1,0},{2,3},{3,2},{4,5},{5,4},{6,7},{7,6},{8,9},{9,8},{10,11... | collective-permute-start | bytes 786440 | tf_op jit(solution)/shard_map/ppermute | solution.py:188
  31.3 19.6 %collective-permute-start.5 = (bf16[512,256]{1,0:T(8,128)(2,1)S(1)}, bf16[512,256]{1,0:T(8,128)(2,1)S(1)}, u32[]{:S(2)}, u32[]{:S(2)}) collective-permute-start(bf16[512,256]{1,0:T(8,128)(2,1)S(1)} %pad_maximum_fusion.4), channel_id=1, source_target_pairs={{16,0},{17,1},{18,2},{19,3},{20,4},{21,5},{22,6},{23,7},{24,8},{25... | collective-permute-start | bytes 786440 | tf_op jit(solution)/shard_map/ppermute | solution.py:188
  51.1 5.3 %collective-permute-start.6 = (bf16[256,256]{1,0:T(8,128)(2,1)S(1)}, bf16[256,256]{1,0:T(8,128)(2,1)S(1)}, u32[]{:S(2)}, u32[]{:S(2)}) collective-permute-start(bf16[256,256]{1,0:T(8,128)(2,1)S(1)} %pad_maximum_fusion.8), channel_id=1, source_target_pairs={{0,8},{1,9},{2,10},{3,11},{4,12},{5,13},{6,14},{7,15},{8,0},{9,1},... | collective-permute-start | bytes 393224 | tf_op jit(solution)/shard_map/ppermute | solution.py:188
  56.4 5.6 %collective-permute-start.7 = (bf16[128,256]{1,0:T(8,128)(2,1)S(1)}, bf16[128,256]{1,0:T(8,128)(2,1)S(1)}, u32[]{:S(2)}, u32[]{:S(2)}) collective-permute-start(bf16[128,256]{1,0:T(8,128)(2,1)S(1)} %slice.91), channel_id=1, source_target_pairs={{0,7},{1,2},{2,1},{3,4},{4,3},{5,6},{6,5},{7,0},{8,15},{9,10},{10,... | collective-permute-start | bytes 196616 | tf_op jit(solution)/shard_map/ppermute | solution.py:188
